TPU v7x, 32 devices: a whole 2x2x4 slice. The times are simulated.
32 devices in a mesh: expert: 8 (over y, x, core), dp: 4 (over z).
Axes of the slice: x: 2, y: 2, z: 4, core: 2. Of those that a mesh axis runs over, the one named last changes fastest.
Arguments:
- tokens: bfloat16 [512, 2048], P(('expert', 'dp')), may hold values from -6 to 6
- out_grad: bfloat16 [512, 2048], P(('expert', 'dp')), may hold values from -6 to 6
- routes: int32 [512, 8], P(('expert', 'dp')), may hold values from 0 to 15, all different within a row; in each aligned block of 16 rows (0 to 15, 16 to 31, ...) at most 16 rows name the same one
- route_gates: float32 [512, 8], P(('expert', 'dp')), may hold values from 0.05 to 0.5
- w_gate: bfloat16 [16, 2048, 384], P('expert'), may hold values from -0.125 to 0.125
- w_up: bfloat16 [16, 2048, 384], P('expert'), may hold values from -0.125 to 0.125
- w_down: bfloat16 [16, 384, 2048], P('expert'), may hold values from -0.3125 to 0.3125
Outputs:
- token_grad: bfloat16 [512, 2048], P(('expert', 'dp'))
- down_grad: float32 [384, 16, 2048], P('dp', 'expert')
Inputs may be any that keep to these rules, and one draw needn't show every extreme that they name: `routes`: each row names 8 different experts. Among the 16 tokens of one device no expert is named more than 16 times, a bound that some block reaches.
All inputs are finite; a program needn't handle non-finite values.
Results may differ from a plain program's by a relative error of at most 0.014.
Values may be sent and summed in bfloat16 or wider, within the bound.
A program may use at most 64 MiB of HBM per device.

v0:
```python
import jax
import jax.numpy as jnp
from jax import lax
from jax.sharding import PartitionSpec as P


def gate_up(arrived, w_gate, w_up):
    gate_pre = jnp.einsum("erd,edf->erf", arrived, w_gate, preferred_element_type=jnp.float32)
    up_pre = jnp.einsum("erd,edf->erf", arrived, w_up, preferred_element_type=jnp.float32)
    return (gate_pre, up_pre)


def shards(tokens, out_grad, routes, route_gates, w_gate, w_up, w_down):
    tok_count, model_width = tokens.shape
    top_count = routes.shape[1]
    local_experts = w_gate.shape[0]
    groups = lax.axis_size("expert")
    experts = local_experts * groups
    slot_count = 2 * tok_count * top_count // experts
    flat_routes = routes.reshape(-1)
    onehot = (flat_routes[:, None] == jnp.arange(experts, dtype=jnp.int32)[None, :]).astype(
        jnp.int32
    )
    slot_rank = jnp.sum(onehot * (jnp.cumsum(onehot, axis=0) - onehot), axis=1)
    slot_index = flat_routes * slot_count + slot_rank
    placement = slot_index[None, :] == jnp.arange(experts * slot_count, dtype=jnp.int32)[:, None]
    route_place = placement.astype(jnp.bfloat16)
    token_place = jnp.sum(
        placement.reshape(experts * slot_count, tok_count, top_count).astype(jnp.float32), axis=2
    ).astype(jnp.bfloat16)
    send_inputs = (
        jnp.dot(token_place, tokens, preferred_element_type=jnp.float32)
        .astype(jnp.bfloat16)
        .reshape(experts, slot_count, model_width)
    )
    scaled = (
        (route_gates[:, :, None] * out_grad[:, None, :].astype(jnp.float32))
        .astype(jnp.bfloat16)
        .reshape(tok_count * top_count, model_width)
    )
    send_grads = (
        jnp.dot(route_place, scaled, preferred_element_type=jnp.float32)
        .astype(jnp.bfloat16)
        .reshape(experts, slot_count, model_width)
    )
    arrived, arrived_grad = (
        lax.all_to_all(send_inputs, "expert", split_axis=0, concat_axis=1, tiled=True),
        lax.all_to_all(send_grads, "expert", split_axis=0, concat_axis=1, tiled=True),
    )
    gate_pre, up_pre = gate_up(arrived, w_gate, w_up)
    sigmoid_gate = jax.nn.sigmoid(gate_pre)
    silu_gate = gate_pre * sigmoid_gate
    hidden = (silu_gate * up_pre).astype(jnp.bfloat16)
    hidden_grad = jnp.einsum(
        "erd,efd->erf", arrived_grad, w_down, preferred_element_type=jnp.float32
    )
    gate_grad = (
        hidden_grad * up_pre * (sigmoid_gate + gate_pre * sigmoid_gate * (1.0 - sigmoid_gate))
    ).astype(jnp.bfloat16)
    up_grad = (hidden_grad * silu_gate).astype(jnp.bfloat16)
    row_grads = (
        jnp.einsum("erf,edf->erd", gate_grad, w_gate, preferred_element_type=jnp.float32)
        + jnp.einsum("erf,edf->erd", up_grad, w_up, preferred_element_type=jnp.float32)
    ).astype(jnp.bfloat16)
    returned = lax.all_to_all(row_grads, "expert", split_axis=1, concat_axis=0, tiled=True)
    token_grad = lax.dot_general(
        token_place,
        returned.reshape(experts * slot_count, model_width),
        (((0,), (0,)), ((), ())),
        preferred_element_type=jnp.float32,
    ).astype(jnp.bfloat16)
    hidden_units = hidden.shape[2]
    share_rows = hidden_units // lax.axis_size("dp")
    partial_grad = jnp.einsum(
        "erf,erd->fed", hidden, arrived_grad, preferred_element_type=jnp.float32
    ).astype(jnp.bfloat16)
    total_grad = lax.psum(partial_grad, "dp").astype(jnp.float32)
    first_row = lax.axis_index("dp") * share_rows
    down_grad = lax.dynamic_slice_in_dim(total_grad, first_row, share_rows, 0)
    return (token_grad, down_grad)


def solution(mesh):
    placed = (
        P(("expert", "dp"), None),
        P(("expert", "dp"), None),
        P(("expert", "dp"), None),
        P(("expert", "dp"), None),
        P("expert", None, None),
        P("expert", None, None),
        P("expert", None, None),
    )
    return jax.shard_map(
        shards,
        mesh=mesh,
        in_specs=placed,
        out_specs=(P(("expert", "dp"), None), P("dp", "expert", None)),
        check_vma=False,
    )
```

profile of v0, /device:TPU:0, one launch (start us, length us, event | category | flops | bytes accessed | tf_op | source)
XLA Modules:
  0.0 193.7 jit_solution(11863418635343941623)
XLA Ops:
  7.2 0.0 copy-start
  7.2 0.0 copy-start.6
  7.2 0.9 copy.42
  8.1 0.1 eq.35
  8.2 0.1 fusion.10
  8.3 0.2 reduce_window_sum.11
  8.5 0.2 select_reduce_fusion
  8.7 0.9 convert_element_type.51
  9.5 0.8 copy.44
  10.3 0.1 mul.63
  10.4 1.5 convolution_convert_fusion.1
  11.8 5.2 %all-to-all-start = ((bf16[16,16,2048]{2,1,0:T(8,128)(2,1)}), bf16[16,16,2048]{2,1,0:T(8,128)(2,1)}, u32[]{:S(2)}, u32[]{:S(2)}) async-start(bf16[16,16,2048]{2,1,0:T(8,128)(2,1)} %bitcast.38), calls=%async_computation | async-start | bytes 2097152 | tf_op jit(solution)/shard_map/all_to_all | solution.py:48
  17.0 0.1 reduce_sum.21
  17.1 0.1 convert_reduce_fusion
  17.3 0.0 copy-done.6
  17.3 1.5 convolution_convert_fusion.2
  18.7 13.8 %all-to-all-done = bf16[16,16,2048]{2,1,0:T(8,128)(2,1)} async-done(((bf16[16,16,2048]{2,1,0:T(8,128)(2,1)}), bf16[16,16,2048]{2,1,0:T(8,128)(2,1)}, u32[]{:S(2)}, u32[]{:S(2)}) %all-to-all-start) | async-done | bytes 1048608 | tf_op jit(solution)/shard_map/all_to_all | solution.py:48
  32.5 4.2 %all-to-all-start.1 = ((bf16[16,16,2048]{2,1,0:T(8,128)(2,1)}), bf16[16,16,2048]{2,1,0:T(8,128)(2,1)}, u32[]{:S(2)}, u32[]{:S(2)}) async-start(bf16[16,16,2048]{2,1,0:T(8,128)(2,1)} %bitcast.39), calls=%async_computation.1 | async-start | bytes 2097152 | tf_op jit(solution)/shard_map/all_to_all | solution.py:47
  36.8 0.0 all-reduce.2.cloned.1.call-start
  36.8 2.3 %copy.45 = bf16[8,2,16,2048]{3,2,0,1:T(8,128)(2,1)} copy(bf16[8,2,16,2048]{3,2,1,0:T(8,128)(2,1)} %bitcast.2) | data formatting | bytes 2097152 | tf_op jit(solution)/shard_map/all_to_all | solution.py:48
  39.1 13.0 %all-to-all-done.1 = bf16[16,16,2048]{2,1,0:T(8,128)(2,1)} async-done(((bf16[16,16,2048]{2,1,0:T(8,128)(2,1)}), bf16[16,16,2048]{2,1,0:T(8,128)(2,1)}, u32[]{:S(2)}, u32[]{:S(2)}) %all-to-all-start.1) | async-done | bytes 1048608 | tf_op jit(solution)/shard_map/all_to_all | solution.py:47
  52.2 0.0 copy-start.1
  52.2 1.5 copy.46
  53.6 0.0 copy-done
  53.7 0.8 fusion.19
  54.4 0.0 copy-done.1
  54.4 0.0 copy-start.3
  54.4 0.7 fusion.18
  55.1 0.0 copy-start.4
  55.2 0.8 copy-done.4
  55.9 0.0 copy-done.3
  55.9 2.7 %fusion = bf16[384,2,2048]{0,2,1:T(8,128)(2,1)} fusion(bf16[2,128,2048]{2,1,0:T(8,128)(2,1)S(1)} %bitcast.35, f32[2,128,384]{2,1,0:T(8,128)S(1)} %fusion.18, f32[2,128,384]{2,1,0:T(8,128)S(1)} %fusion.19), kind=kOutput, calls=%fused_computation.1 | convolution fusion | flops 404815872 | bytes 4980736 | tf_op jit(solution)/shard_map/erf,erd->fed/dot_general | solution.py:74
  58.6 0.0 all-reduce.2.cloned.1.call-update
  58.6 0.0 copy-start.5
  58.7 3.3 %fusion.17 = f32[2,128,384]{2,1,0:T(8,128)S(1)} fusion(bf16[2,128,2048]{2,1,0:T(8,128)(2,1)} %bitcast.34, bf16[2,384,2048]{2,1,0:T(8,128)(2,1)} %param.13), kind=kOutput, calls=%fused_computation.31 | convolution fusion | flops 402653184 | bytes 4587520 | tf_op jit(solution)/shard_map/erd,efd->erf/dot_general | solution.py:54
  62.0 0.0 copy-done.5
  62.0 0.0 copy-start.2
  62.0 1.1 fusion.7
  63.1 0.8 copy-done.2
  63.9 1.1 fusion.1
  65.0 2.0 %copy.47 = bf16[2,128,2048]{2,0,1:T(2,128)(2,1)} copy(bf16[2,128,2048]{2,1,0:T(8,128)(2,1)S(1)} %fusion.1) | data formatting | bytes 2097152 | tf_op jit(solution)/shard_map/convert_element_type | solution.py:64
  67.1 4.2 %all-to-all-start.2 = ((bf16[2,128,2048]{2,0,1:T(2,128)(2,1)}), bf16[2,128,2048]{2,0,1:T(2,128)(2,1)}, u32[]{:S(2)}, u32[]{:S(2)}) async-start(bf16[2,128,2048]{2,0,1:T(2,128)(2,1)} %copy.47), calls=%async_computation.2 | async-start | bytes 2097152 | tf_op jit(solution)/shard_map/all_to_all | solution.py:65
  71.3 15.4 %all-to-all-done.2 = bf16[2,128,2048]{2,0,1:T(2,128)(2,1)} async-done(((bf16[2,128,2048]{2,0,1:T(2,128)(2,1)}), bf16[2,128,2048]{2,0,1:T(2,128)(2,1)}, u32[]{:S(2)}, u32[]{:S(2)}) %all-to-all-start.2) | async-done | bytes 1048608 | tf_op jit(solution)/shard_map/all_to_all | solution.py:65
  86.7 1.6 copy.48
  88.3 0.1 copy.49
  88.4 0.9 convolution_convert_fusion.3
  89.3 90.4 %all-reduce.2.cloned.1.call-done = bf16[384,2,2048]{0,2,1:T(8,128)(2,1)} async-done(((bf16[384,2,2048]{0,2,1:T(8,128)(2,1)}), bf16[384,2,2048]{0,2,1:T(8,128)(2,1)}) %all-reduce.2.cloned.1.call-update) | async-done | bytes 3145744 | tf_op jit(solution)/shard_map/psum | solution.py:77
  179.7 3.3 %dynamic-slice_convert_fusion = f32[96,2,2048]{0,2,1:T(8,128)} fusion(bf16[384,2,2048]{0,2,1:T(8,128)(2,1)} %all-reduce.2.cloned.1.call-done, s32[]{:T(128)S(6)} %select_n.3), kind=kLoop, calls=%fused_computation.7 | loop fusion | flops 393216 | bytes 2359300 | tf_op jit(solution)/shard_map/convert_element_type | solution.py:77
  183.0 3.9 %copy.51 = f32[96,2,2048]{2,1,0:T(2,128)} copy(f32[96,2,2048]{0,2,1:T(8,128)} %dynamic-slice_convert_fusion) | data formatting | bytes 3145728
  (2 shorter events, 0.0 us)
Async XLA Ops:
  7.2 46.5 %copy-start = (bf16[2,2048,384]{2,1,0:T(8,128)(2,1)S(1)}, bf16[2,2048,384]{2,1,0:T(8,128)(2,1)}, u32[]{:S(2)}) copy-start(bf16[2,2048,384]{2,1,0:T(8,128)(2,1)} %param.11) | copy-start | bytes 9437188
  7.2 10.1 %copy-start.6 = (bf16[16,2048]{1,0:T(8,128)(2,1)S(1)}, bf16[16,2048]{1,0:T(8,128)(2,1)}, u32[]{:S(2)}) copy-start(bf16[16,2048]{1,0:T(8,128)(2,1)} %param.7) | copy-start | bytes 196612
  11.8 20.7 %all-to-all-start = ((bf16[16,16,2048]{2,1,0:T(8,128)(2,1)}), bf16[16,16,2048]{2,1,0:T(8,128)(2,1)}, u32[]{:S(2)}, u32[]{:S(2)}) async-start(bf16[16,16,2048]{2,1,0:T(8,128)(2,1)} %bitcast.38), calls=%async_computation | async-start | bytes 2097152 | tf_op jit(solution)/shard_map/all_to_all | solution.py:48
  32.5 19.6 %all-to-all-start.1 = ((bf16[16,16,2048]{2,1,0:T(8,128)(2,1)}), bf16[16,16,2048]{2,1,0:T(8,128)(2,1)}, u32[]{:S(2)}, u32[]{:S(2)}) async-start(bf16[16,16,2048]{2,1,0:T(8,128)(2,1)} %bitcast.39), calls=%async_computation.1 | async-start | bytes 2097152 | tf_op jit(solution)/shard_map/all_to_all | solution.py:47
  36.8 142.9 %all-reduce.2.cloned.1.call-start = ((), (), s32[]{:S(2)}) async-start(), calls=%async_computation.3 | async-start | bytes 6291456 | tf_op jit(solution)/shard_map/psum | solution.py:77
  52.2 2.3 %copy-start.1 = (bf16[2,2048,384]{2,1,0:T(8,128)(2,1)S(1)}, bf16[2,2048,384]{2,1,0:T(8,128)(2,1)}, u32[]{:S(2)}) copy-start(bf16[2,2048,384]{2,1,0:T(8,128)(2,1)} %param.12) | copy-start | bytes 9437188
  54.4 1.5 copy-start.3
  55.1 0.8 copy-start.4
  58.6 3.3 %copy-start.5 = (f32[2,128,384]{2,1,0:T(8,128)S(1)}, f32[2,128,384]{2,1,0:T(8,128)}, u32[]{:S(2)}) copy-start(f32[2,128,384]{2,1,0:T(8,128)} %copy-done.4) | copy-start | bytes 1179652
  62.0 1.9 copy-start.2
  67.1 19.6 %all-to-all-start.2 = ((bf16[2,128,2048]{2,0,1:T(2,128)(2,1)}), bf16[2,128,2048]{2,0,1:T(2,128)(2,1)}, u32[]{:S(2)}, u32[]{:S(2)}) async-start(bf16[2,128,2048]{2,0,1:T(2,128)(2,1)} %copy.47), calls=%async_computation.2 | async-start | bytes 2097152 | tf_op jit(solution)/shard_map/all_to_all | solution.py:65
Sparse Core Ops, SparseCore 0:
  58.8 120.8 all-reduce.1
where the time goes:
time: 194 us
  waiting for transfers between devices  133 us (69%)
  local copies, waits for them, and re-layouts  14.9 us (8%)
  between operations  14.2 us (7%)
  starting transfers between devices  13.7 us (7%)
  matrix products  13.5 us (7%)
  other arithmetic  4.72 us (2%)
    psum x1, waiting for transfers between devices, shards(): total_grad = lax.psum(partial_grad, 'dp').astype(jnp.float32)  90.4 us
    all_to_all x1, waiting for transfers between devices, shards(): lax.all_to_all(row_grads, 'expert', split_axis=1, concat_axis=0, tiled=True)  15.4 us
    all_to_all x1, waiting for transfers between devices, shards(): lax.all_to_all(send_grads, 'expert', split_axis=0, concat_axis=1, tiled=T...  13.8 us
    all_to_all x1, waiting for transfers between devices, shards(): lax.all_to_all(send_inputs, 'expert', split_axis=0, concat_axis=1, tiled=...  13 us
    unnamed x17, local copies, waits for them, and re-layouts  7.11 us
    all_to_all x1, starting transfers between devices, shards(): lax.all_to_all(send_grads, 'expert', split_axis=0, concat_axis=1, tiled=T...  5.2 us
    all_to_all x1, starting transfers between devices, shards(): lax.all_to_all(row_grads, 'expert', split_axis=1, concat_axis=0, tiled=True)  4.25 us
    all_to_all x1, starting transfers between devices, shards(): lax.all_to_all(send_inputs, 'expert', split_axis=0, concat_axis=1, tiled=...  4.24 us
  transfers between devices with their start and end apart: 4, of which 4 were waited for; matrix products, arithmetic and copies ran while one was open for 7% of the time, Pallas kernels for 0%

commit v1 on v0

--- a/solution.py
+++ b/solution.py
@@ -1,7 +1,14 @@
+import functools
+
 import jax
 import jax.numpy as jnp
 from jax import lax
+from jax.experimental import pallas as pl
+from jax.experimental.pallas import tpu as pltpu
 from jax.sharding import PartitionSpec as P
+
+VMEM_BUDGET = 44 << 20
+NT = (((1,), (1,)), ((), ()))
 
 
 def gate_up(arrived, w_gate, w_up):
@@ -10,7 +17,7 @@
     return (gate_pre, up_pre)
 
 
-def shards(tokens, out_grad, routes, route_gates, w_gate, w_up, w_down):
+def collective_shards(tokens, out_grad, routes, route_gates, w_gate, w_up, w_down):
     tok_count, model_width = tokens.shape
     top_count = routes.shape[1]
     local_experts = w_gate.shape[0]
@@ -80,6 +87,294 @@
     return (token_grad, down_grad)
 
 
+def flip(index, bits):
+    out, step = index, 1
+    while step <= bits:
+        if bits & step:
+            out = out + step * (1 - 2 * ((index // step) % 2))
+        step *= 2
+    return out
+
+
+def copy_keys(chips, planes, local_experts, parts):
+    keys = []
+    for name in ("x", "r", "g"):
+        keys += [(name, d) for d in range(1, chips)] + [(name + "c", d) for d in range(chips)]
+    keys += [("z", k) for k in range(1, planes)]
+    keys += [("d", k, d) for k in range(planes) for d in range(1, chips)]
+    keys += [("dc", k, d) for k in range(planes) for d in range(chips)]
+    keys += [("h", k, e) for k in range(1, planes) for e in range(local_experts)]
+    keys += [("p", j) for j in range(parts)]
+    keys += [("t", j, d) for j in range(parts) for d in range(1, chips)]
+    return {key: i for i, key in enumerate(keys)}
+
+
+def fused_kernel(
+    chips, planes, parts, tok, dy, rt, gt, wg, wu, wd, token_out, down_out,
+    xb, db, rb, gb, wgv, wuv, wdv, gates, ups, hid_out, hid_in, grads_g, grads_u,
+    keep, pair_out, pair_in, ret_out, ret_in, lsem, ssem, rsem,
+):
+    local_experts, model_width, hidden_units = wg.shape
+    rows = tok.shape[0]
+    count = 2 * chips * rows
+    share = hidden_units // planes
+    width = model_width // parts
+    me, plane = lax.axis_index("expert"), lax.axis_index("dp")
+    chip, core = me // 2, me % 2
+    partner = {"expert": chip * 2 + 1 - core, "dp": plane}
+    across = [{"expert": flip(chip, d) * 2 + core, "dp": plane} for d in range(chips)]
+    above = [{"expert": me, "dp": flip(plane, k)} for k in range(planes)]
+    keys = copy_keys(chips, planes, local_experts, parts)
+
+    local = []
+
+    def load(src, dst):
+        c = pltpu.make_async_copy(src, dst, lsem.at[len(local)])
+        c.start()
+        local.append(c)
+        return c
+
+    own = [load(tok, xb.at[0]), load(rt, rb.at[0]), load(gt, gb.at[0]), load(dy, db.at[0, 0])]
+    gate_up_loads = [(load(wg.at[e], wgv.at[e]), load(wu.at[e], wuv.at[e])) for e in range(local_experts)]
+    down_loads = [load(wd.at[e], wdv.at[e]) for e in range(local_experts)]
+
+    def remote(key, src, dst, target):
+        i = keys[key]
+        return pltpu.make_async_remote_copy(
+            src_ref=src, dst_ref=dst, send_sem=ssem.at[i], recv_sem=rsem.at[i],
+            device_id=target, device_id_type=pl.DeviceIdType.MESH,
+        )
+
+    copies = {}
+    for name, src, buf in (("x", tok, xb), ("r", rt, rb), ("g", gt, gb)):
+        for d in range(chips):
+            if d:
+                copies[name, d] = remote((name, d), src, buf.at[2 * d], across[d])
+            copies[name + "c", d] = remote(
+                (name + "c", d), buf.at[2 * d] if d else src, buf.at[2 * d + 1], partner
+            )
+    for k in range(planes):
+        if k:
+            copies["z", k] = remote(("z", k), dy, db.at[k, 0], above[k])
+        block = db.at[k, 0] if k else dy
+        for d in range(chips):
+            if d:
+                copies["d", k, d] = remote(("d", k, d), block, db.at[k, 2 * d], across[d])
+            copies["dc", k, d] = remote(
+                ("dc", k, d), db.at[k, 2 * d] if d else block, db.at[k, 2 * d + 1], partner
+            )
+    for k in range(1, planes):
+        first = pl.multiple_of(flip(plane, k) * share, 16)
+        for e in range(local_experts):
+            copies["h", k, e] = remote(
+                ("h", k, e), hid_out.at[e, pl.ds(first, share)], hid_in.at[k, e], above[k]
+            )
+    for j in range(parts):
+        copies["p", j] = remote(("p", j), pair_out.at[j], pair_in.at[j], partner)
+        for d in range(1, chips):
+            copies["t", j, d] = remote(("t", j, d), ret_out.at[j, d], ret_in.at[j, d], across[d])
+
+    barrier = pltpu.get_barrier_semaphore()
+    targets = [partner] + across[1:] + above[1:]
+    for target in targets:
+        pl.semaphore_signal(barrier, inc=1, device_id=target, device_id_type=pl.DeviceIdType.MESH)
+    pl.semaphore_wait(barrier, len(targets))
+
+    for name in ("x", "r", "g"):
+        for d in range(1, chips):
+            copies[name, d].start()
+    for k in range(planes - 1, 0, -1):
+        copies["z", k].start()
+    for d in range(1, chips):
+        copies["d", 0, d].start()
+    for name in ("x", "r", "g"):
+        copies[name + "c", 0].start()
+    copies["dc", 0, 0].start()
+
+    for d in range(1, chips):
+        for name in ("x", "r", "g"):
+            copies[name, d].wait_recv()
+            copies[name + "c", d].start()
+    for c in own:
+        c.wait()
+    for d in range(chips):
+        for name in ("x", "r", "g"):
+            copies[name + "c", d].wait_recv()
+
+    x = xb[...].reshape(count, model_width)
+    for e in range(local_experts):
+        for c in gate_up_loads[e]:
+            c.wait()
+        gates[e] = jnp.dot(x, wgv[e], preferred_element_type=jnp.float32)
+        ups[e] = jnp.dot(x, wuv[e], preferred_element_type=jnp.float32)
+        if e == 0:
+            for d in range(1, chips):
+                copies["d", 0, d].wait_recv()
+                copies["dc", 0, d].start()
+    for k in range(1, planes):
+        copies["z", k].wait_recv()
+        for d in range(1, chips):
+            copies["d", k, d].start()
+        copies["dc", k, 0].start()
+    for d in range(chips):
+        copies["dc", 0, d].wait_recv()
+
+    named = rb[...].reshape(count, rb.shape[2])
+    given = gb[...].reshape(count, gb.shape[2])
+    grad_rows = db[0].reshape(count, model_width)
+    for e in range(local_experts):
+        down_loads[e].wait()
+        gain = jnp.sum(
+            jnp.where(named == me * local_experts + e, given, 0.0), axis=1, keepdims=True
+        )
+        hidden_grad = gain * lax.dot_general(
+            grad_rows, wdv[e], NT, preferred_element_type=jnp.float32
+        )
+        gate_pre, up_pre = gates[e], ups[e]
+        s = jax.nn.sigmoid(gate_pre)
+        silu = gate_pre * s
+        hid_out[e] = (silu * up_pre * gain).T.astype(jnp.bfloat16)
+        grads_g[e] = (hidden_grad * up_pre * (s + gate_pre * s * (1.0 - s))).astype(jnp.bfloat16)
+        grads_u[e] = (hidden_grad * silu).astype(jnp.bfloat16)
+    for k in range(1, planes):
+        for e in range(local_experts):
+            copies["h", k, e].start()
+
+    for j in range(parts):
+        cols = pl.ds(j * width, width)
+        total = None
+        for e in range(local_experts):
+            for grads, weights in ((grads_g, wgv), (grads_u, wuv)):
+                term = lax.dot_general(
+                    grads[e], weights[e, cols, :], NT, preferred_element_type=jnp.float32
+                )
+                total = term if total is None else total + term
+        total = total.reshape(chips, 2, rows, width)
+        keep[j] = total[:, 0]
+        pair_out[j] = total[:, 1].astype(jnp.bfloat16)
+        copies["p", j].start()
+
+    for k in range(1, planes):
+        for d in range(1, chips):
+            copies["d", k, d].wait_recv()
+            copies["dc", k, d].start()
+
+    for j in range(parts):
+        copies["p", j].wait_recv()
+        total = keep[j] + pair_in[j].astype(jnp.float32)
+        keep[j, 0] = total[0]
+        for d in range(1, chips):
+            ret_out[j, d] = total[d].astype(jnp.bfloat16)
+        for d in range(1, chips):
+            copies["t", j, d].start()
+
+    first = pl.multiple_of(plane * share, 16)
+    for k in range(1, planes):
+        for e in range(local_experts):
+            copies["h", k, e].wait_recv()
+        for d in range(chips):
+            copies["dc", k, d].wait_recv()
+    every = db[...].reshape(planes * count, model_width)
+    for e in range(local_experts):
+        pieces = [hid_out[e, pl.ds(first, share), :]] + [hid_in[k, e] for k in range(1, planes)]
+        down_out[e] = jnp.dot(
+            jnp.concatenate(pieces, axis=1), every, preferred_element_type=jnp.float32
+        )
+
+    for j in range(parts):
+        total = keep[j, 0]
+        for d in range(1, chips):
+            copies["t", j, d].wait_recv()
+            total = total + ret_in[j, d].astype(jnp.float32)
+        token_out[:, pl.ds(j * width, width)] = total.astype(jnp.bfloat16)
+    for c in copies.values():
+        c.wait_send()
+
+
+def fused_shapes(chips, planes, parts, rows, top, local_experts, model_width, hidden_units):
+    bf16, f32 = jnp.bfloat16, jnp.float32
+    count, width = 2 * chips * rows, model_width // parts
+    return [
+        ((2 * chips, rows, model_width), bf16),
+        ((planes, 2 * chips, rows, model_width), bf16),
+        ((2 * chips, rows, top), jnp.int32),
+        ((2 * chips, rows, top), f32),
+        ((local_experts, model_width, hidden_units), bf16),
+        ((local_experts, model_width, hidden_units), bf16),
+        ((local_experts, hidden_units, model_width), bf16),
+        ((local_experts, count, hidden_units), f32),
+        ((local_experts, count, hidden_units), f32),
+        ((local_experts, hidden_units, count), bf16),
+        ((planes, local_experts, hidden_units // planes, count), bf16),
+        ((local_experts, count, hidden_units), bf16),
+        ((local_experts, count, hidden_units), bf16),
+        ((parts, chips, rows, width), f32),
+        ((parts, chips, rows, width), bf16),
+        ((parts, chips, rows, width), bf16),
+        ((parts, chips, rows, width), bf16),
+        ((parts, chips, rows, width), bf16),
+    ]
+
+
+def buffer_bytes(shapes):
+    total = 0
+    for dims, kind in shapes:
+        size = jnp.dtype(kind).itemsize
+        for dim in dims[:-1]:
+            size *= dim
+        total += size * (-(-dims[-1] // 128) * 128)
+    return total
+
+
+def plan(tokens, routes, w_gate):
+    groups, planes = lax.axis_size("expert"), lax.axis_size("dp")
+    chips, parts = groups // 2, 2
+    rows, model_width = tokens.shape
+    local_experts, _, hidden_units = w_gate.shape
+    if groups % 2 or chips & (chips - 1) or planes & (planes - 1):
+        return None
+    if rows % 16 or hidden_units % (16 * planes) or (groups * rows) % 128 or model_width % (128 * parts):
+        return None
+    shapes = fused_shapes(
+        chips, planes, parts, rows, routes.shape[1], local_experts, model_width, hidden_units
+    )
+    if buffer_bytes(shapes) > VMEM_BUDGET:
+        return None
+    return chips, planes, parts, shapes
+
+
+def shards(tokens, out_grad, routes, route_gates, w_gate, w_up, w_down):
+    planned = plan(tokens, routes, w_gate)
+    if planned is None:
+        return collective_shards(tokens, out_grad, routes, route_gates, w_gate, w_up, w_down)
+    chips, planes, parts, shapes = planned
+    rows, model_width = tokens.shape
+    local_experts, _, hidden_units = w_gate.shape
+    share = hidden_units // planes
+    amount = len(copy_keys(chips, planes, local_experts, parts))
+    vmem = pl.BlockSpec(memory_space=pltpu.VMEM)
+    token_grad, down_grad = pl.pallas_call(
+        functools.partial(fused_kernel, chips, planes, parts),
+        out_shape=(
+            jax.ShapeDtypeStruct((rows, model_width), jnp.bfloat16),
+            jax.ShapeDtypeStruct((local_experts, share, model_width), jnp.float32),
+        ),
+        in_specs=[pl.BlockSpec(memory_space=pl.ANY)] * 7,
+        out_specs=(vmem, vmem),
+        scratch_shapes=[pltpu.VMEM(dims, kind) for dims, kind in shapes]
+        + [
+            pltpu.SemaphoreType.DMA((4 + 3 * local_experts,)),
+            pltpu.SemaphoreType.DMA((amount,)),
+            pltpu.SemaphoreType.DMA((amount,)),
+        ],
+        compiler_params=pltpu.CompilerParams(
+            collective_id=0, has_side_effects=True, vmem_limit_bytes=60 << 20
+        ),
+        name="expert_backward",
+    )(tokens, out_grad, routes, route_gates, w_gate, w_up, w_down)
+    return (token_grad, down_grad.transpose(1, 0, 2))
+
+
 def solution(mesh):
     placed = (
         P(("expert", "dp"), None),

time: 194 us -> 41.6 us (0.21)
  waiting for transfers between devices: 133 us -> 0 us
  Pallas kernels: 0 us -> 33.6 us
  starting transfers between devices: 13.7 us -> 0 us
  between operations: 14.2 us -> 0.65 us
  matrix products: 13.5 us -> 0 us
  local copies, waits for them, and re-layouts: 14.9 us -> 7.14 us
  other arithmetic: 4.72 us -> 0 us
    psum x1 -> x0, waiting for transfers between devices: 90.4 us -> none  [shards(): total_grad = lax.psum(partial_grad, 'dp').astype(jnp.float32)]
    all_to_all x3 -> x0, waiting for transfers between devices: 42.2 us -> none  [the longest x1 15.4 us: shards(): lax.all_to_all(row_grads, 'expert', split_axis=1, concat_axis=0, tiled=True)]
    pallas_call x0 -> x1, Pallas kernels: none -> 33.6 us  [shards(): pl.pallas_call(functools.partial(fused_kernel, chips, planes, parts), out...]
    all_to_all x3 -> x0, starting transfers between devices: 13.7 us -> none  [the longest x1 5.2 us: shards(): lax.all_to_all(send_grads, 'expert', split_axis=0, concat_axis=1, tiled=T...]
    dot_general x9 -> x0, matrix products: 13.5 us -> none  [the longest x1 3.32 us: shards(): jnp.einsum('erd,efd->erf', arrived_grad, w_down, preferred_element_type=j...]
    all_to_all x4 -> x0, local copies, waits for them, and re-layouts: 5.45 us -> none  [the longest x1 2.3 us: shards(): lax.all_to_all(send_grads, 'expert', split_axis=0, concat_axis=1, tiled=T...]
    convert_element_type x3 -> x0, other arithmetic: 4.24 us -> none  [the longest x1 3.29 us: shards(): total_grad = lax.psum(partial_grad, 'dp').astype(jnp.float32)]
    convert_element_type x1 -> x0, local copies, waits for them, and re-layouts: 2.05 us -> none  [shards(): row_grads = (jnp.einsum('erf,edf->erd', gate_grad, w_gate, preferred_elem...]
  transfers between devices with their start and end apart: 4 -> 0, of which waited for: 4 -> 0; matrix products, arithmetic and copies ran while one was open for 7% -> 0% of each run, Pallas kernels for 0% -> 0%
where the time goes in v1:
time: 41.6 us; the launch traced here: 41.4 us
  Pallas kernels  33.6 us (81%)
  local copies, waits for them, and re-layouts  7.14 us (17%)
  between operations  0.65 us (2%)
    pallas_call x1, Pallas kernels, shards(): pl.pallas_call(functools.partial(fused_kernel, chips, planes, parts), out...  33.6 us
    unnamed x6, local copies, waits for them, and re-layouts  7.14 us

profile of v1, /device:TPU:0, one launch (start us, length us, event | category | flops | bytes accessed | tf_op | source)
XLA Modules:
  0.0 41.4 jit_solution(10989146108761835585)
XLA Ops:
  0.6 1.4 %copy.9.rt = s32[16,8]{1,0:T(8,128)} copy(s32[16,8]{0,1:T(8,128)} %param.9) | data formatting | bytes 1024 | tf_op args[2]
  2.0 1.4 %copy.10.gt = f32[16,8]{1,0:T(8,128)} copy(f32[16,8]{0,1:T(8,128)} %param.10) | data formatting | bytes 1024 | tf_op args[3]
  3.3 33.6 %expert_backward.1 = (bf16[16,2048]{1,0:T(8,128)(2,1)}, f32[2,96,2048]{2,1,0:T(8,128)}) custom-call(bf16[16,2048]{1,0:T(8,128)(2,1)} %tok.1, bf16[16,2048]{1,0:T(8,128)(2,1)} %dy.1, s32[16,8]{1,0:T(8,128)} %copy.9.rt, f32[16,8]{1,0:T(8,128)} %copy.10.gt, bf16[2,2048,384]{2,1,0:T(8,128)(2,1)} %wg.1, bf16[2,2048,384]{2,1,0:T(8,128)(2,1)} %wu.1, ...), custom_call_target="tpu_custom_call" | custom-call | tf_op jit(solution)/shard_map/expert_backward/pallas_call | solution.py:356
  36.9 0.0 copy-start
  36.9 3.8 %copy.11 = f32[96,2,2048]{2,1,0:T(2,128)} copy(f32[96,2,2048]{2,0,1:T(8,128)} %bitcast.1) | data formatting | bytes 3145728
  40.7 0.0 copy-done
  40.7 0.6 %copy.13 = bf16[16,2048]{1,0:T(8,128)(2,1)} copy(bf16[16,2048]{1,0:T(8,128)(2,1)S(1)} %copy-done) | data formatting | bytes 131072
Async XLA Ops:
  36.9 3.8 %copy-start = (bf16[16,2048]{1,0:T(8,128)(2,1)S(1)}, bf16[16,2048]{1,0:T(8,128)(2,1)}, u32[]{:S(2)}) copy-start(bf16[16,2048]{1,0:T(8,128)(2,1)} %get-tuple-element.10) | copy-start | bytes 196612

commit v2 on v1

--- a/solution.py
+++ b/solution.py
@@ -8,6 +8,7 @@
 from jax.sharding import PartitionSpec as P
 
 VMEM_BUDGET = 44 << 20
+STEPS = 4
 NT = (((1,), (1,)), ((), ()))
 
 
@@ -110,9 +111,9 @@
 
 
 def fused_kernel(
-    chips, planes, parts, tok, dy, rt, gt, wg, wu, wd, token_out, down_out,
-    xb, db, rb, gb, wgv, wuv, wdv, gates, ups, hid_out, hid_in, grads_g, grads_u,
-    keep, pair_out, pair_in, ret_out, ret_in, lsem, ssem, rsem,
+    chips, planes, parts, tok, dy, rt, gt, wg, wu, wd, every, hid_in, own_sum, ret_in,
+    xb, db, rb, gb, wgv, wuv, wdv, gates, ups, hid_out, grads_g, grads_u,
+    keep, pair_out, pair_in, ret_out, lsem, ssem, rsem,
 ):
     local_experts, model_width, hidden_units = wg.shape
     rows = tok.shape[0]
@@ -134,7 +135,7 @@
         local.append(c)
         return c
 
-    own = [load(tok, xb.at[0]), load(rt, rb.at[0]), load(gt, gb.at[0]), load(dy, db.at[0, 0])]
+    own = [load(tok, xb.at[0]), load(rt, rb.at[0]), load(gt, gb.at[0]), load(dy, db.at[0])]
     gate_up_loads = [(load(wg.at[e], wgv.at[e]), load(wu.at[e], wuv.at[e])) for e in range(local_experts)]
     down_loads = [load(wd.at[e], wdv.at[e]) for e in range(local_experts)]
 
@@ -154,14 +155,17 @@
                 (name + "c", d), buf.at[2 * d] if d else src, buf.at[2 * d + 1], partner
             )
     for k in range(planes):
+        blocks = every.at[k] if k else db
         if k:
-            copies["z", k] = remote(("z", k), dy, db.at[k, 0], above[k])
-        block = db.at[k, 0] if k else dy
+            copies["z", k] = remote(("z", k), dy, blocks.at[0], above[k])
+        first = blocks.at[0] if k else dy
         for d in range(chips):
-            if d:
-                copies["d", k, d] = remote(("d", k, d), block, db.at[k, 2 * d], across[d])
+            if k and d == chips - 1:
+                copies["d", k, d] = remote(("d", k, d), db.at[2 * d], blocks.at[2 * d], above[k])
+            elif d:
+                copies["d", k, d] = remote(("d", k, d), first, blocks.at[2 * d], across[d])
             copies["dc", k, d] = remote(
-                ("dc", k, d), db.at[k, 2 * d] if d else block, db.at[k, 2 * d + 1], partner
+                ("dc", k, d), blocks.at[2 * d] if d else first, blocks.at[2 * d + 1], partner
             )
     for k in range(1, planes):
         first = pl.multiple_of(flip(plane, k) * share, 16)
@@ -172,7 +176,9 @@
     for j in range(parts):
         copies["p", j] = remote(("p", j), pair_out.at[j], pair_in.at[j], partner)
         for d in range(1, chips):
-            copies["t", j, d] = remote(("t", j, d), ret_out.at[j, d], ret_in.at[j, d], across[d])
+            copies["t", j, d] = remote(
+                ("t", j, d), ret_out.at[j, d], ret_in.at[d - 1, :, pl.ds(j * width, width)], across[d]
+            )
 
     barrier = pltpu.get_barrier_semaphore()
     targets = [partner] + across[1:] + above[1:]
@@ -211,22 +217,28 @@
             for d in range(1, chips):
                 copies["d", 0, d].wait_recv()
                 copies["dc", 0, d].start()
-    for k in range(1, planes):
-        copies["z", k].wait_recv()
-        for d in range(1, chips):
-            copies["d", k, d].start()
-        copies["dc", k, 0].start()
+            for k in range(1, planes):
+                copies["d", k, chips - 1].start()
+            for k in range(1, planes):
+                copies["z", k].wait_recv()
+                for d in range(1, chips - 1):
+                    copies["d", k, d].start()
+                copies["dc", k, 0].start()
     for d in range(chips):
         copies["dc", 0, d].wait_recv()
-
-    named = rb[...].reshape(count, rb.shape[2])
-    given = gb[...].reshape(count, gb.shape[2])
-    grad_rows = db[0].reshape(count, model_width)
+    load(db, every.at[0])
+
+    named, given = rb[...], gb[...]
+    diagonal = lax.broadcasted_iota(jnp.int32, (1, rows, rows), 1) == lax.broadcasted_iota(
+        jnp.int32, (1, rows, rows), 2
+    )
+    grad_rows = db[...].reshape(count, model_width)
     for e in range(local_experts):
         down_loads[e].wait()
         gain = jnp.sum(
             jnp.where(named == me * local_experts + e, given, 0.0), axis=1, keepdims=True
         )
+        gain = jnp.sum(jnp.where(diagonal, gain, 0.0), axis=2, keepdims=True).reshape(count, 1)
         hidden_grad = gain * lax.dot_general(
             grad_rows, wdv[e], NT, preferred_element_type=jnp.float32
         )
@@ -239,6 +251,9 @@
     for k in range(1, planes):
         for e in range(local_experts):
             copies["h", k, e].start()
+    first = pl.multiple_of(plane * share, 16)
+    for e in range(local_experts):
+        load(hid_out.at[e, pl.ds(first, share)], hid_in.at[0, e])
 
     for j in range(parts):
         cols = pl.ds(j * width, width)
@@ -263,32 +278,41 @@
         copies["p", j].wait_recv()
         total = keep[j] + pair_in[j].astype(jnp.float32)
         keep[j, 0] = total[0]
+        load(keep.at[j, 0], own_sum.at[:, pl.ds(j * width, width)])
         for d in range(1, chips):
             ret_out[j, d] = total[d].astype(jnp.bfloat16)
         for d in range(1, chips):
             copies["t", j, d].start()
 
-    first = pl.multiple_of(plane * share, 16)
     for k in range(1, planes):
         for e in range(local_experts):
             copies["h", k, e].wait_recv()
         for d in range(chips):
             copies["dc", k, d].wait_recv()
-    every = db[...].reshape(planes * count, model_width)
-    for e in range(local_experts):
-        pieces = [hid_out[e, pl.ds(first, share), :]] + [hid_in[k, e] for k in range(1, planes)]
-        down_out[e] = jnp.dot(
-            jnp.concatenate(pieces, axis=1), every, preferred_element_type=jnp.float32
-        )
-
     for j in range(parts):
-        total = keep[j, 0]
         for d in range(1, chips):
             copies["t", j, d].wait_recv()
-            total = total + ret_in[j, d].astype(jnp.float32)
-        token_out[:, pl.ds(j * width, width)] = total.astype(jnp.bfloat16)
+    for c in local[len(own) + 3 * local_experts :]:
+        c.wait()
     for c in copies.values():
         c.wait_send()
+
+
+def finish_kernel(every, hid, own_sum, returned, token_out, down_out):
+    planes, local_experts, share, _ = hid.shape
+    blocks = every.shape[1] // 128
+    lines = down_out.reshape(share * blocks * local_experts, 128)
+    for e in range(local_experts):
+        pieces = jnp.concatenate([hid[k, e] for k in range(planes)], axis=1)
+        result = jnp.dot(pieces, every[...], preferred_element_type=jnp.float32)
+        for b in range(blocks):
+            lines[pl.ds(b * local_experts + e, share, stride=blocks * local_experts), :] = (
+                result[:, b * 128 : (b + 1) * 128]
+            )
+    total = own_sum[...]
+    for d in range(returned.shape[0]):
+        total = total + returned[d].astype(jnp.float32)
+    token_out[...] = total.astype(jnp.bfloat16)
 
 
 def fused_shapes(chips, planes, parts, rows, top, local_experts, model_width, hidden_units):
@@ -296,20 +320,18 @@
     count, width = 2 * chips * rows, model_width // parts
     return [
         ((2 * chips, rows, model_width), bf16),
-        ((planes, 2 * chips, rows, model_width), bf16),
-        ((2 * chips, rows, top), jnp.int32),
-        ((2 * chips, rows, top), f32),
+        ((2 * chips, rows, model_width), bf16),
+        ((2 * chips, top, rows), jnp.int32),
+        ((2 * chips, top, rows), f32),
         ((local_experts, model_width, hidden_units), bf16),
         ((local_experts, model_width, hidden_units), bf16),
         ((local_experts, hidden_units, model_width), bf16),
         ((local_experts, count, hidden_units), f32),
         ((local_experts, count, hidden_units), f32),
         ((local_experts, hidden_units, count), bf16),
-        ((planes, local_experts, hidden_units // planes, count), bf16),
         ((local_experts, count, hidden_units), bf16),
         ((local_experts, count, hidden_units), bf16),
         ((parts, chips, rows, width), f32),
-        ((parts, chips, rows, width), bf16),
         ((parts, chips, rows, width), bf16),
         ((parts, chips, rows, width), bf16),
         ((parts, chips, rows, width), bf16),
@@ -333,7 +355,7 @@
     local_experts, _, hidden_units = w_gate.shape
     if groups % 2 or chips & (chips - 1) or planes & (planes - 1):
         return None
-    if rows % 16 or hidden_units % (16 * planes) or (groups * rows) % 128 or model_width % (128 * parts):
+    if rows % 16 or hidden_units % (16 * planes) or (groups * rows) % 128 or model_width % (512 * STEPS):
         return None
     shapes = fused_shapes(
         chips, planes, parts, rows, routes.shape[1], local_experts, model_width, hidden_units
@@ -352,18 +374,21 @@
     local_experts, _, hidden_units = w_gate.shape
     share = hidden_units // planes
     amount = len(copy_keys(chips, planes, local_experts, parts))
-    vmem = pl.BlockSpec(memory_space=pltpu.VMEM)
-    token_grad, down_grad = pl.pallas_call(
+    count = 2 * chips * rows
+    anywhere = pl.BlockSpec(memory_space=pl.ANY)
+    every, hid, own_sum, returned = pl.pallas_call(
         functools.partial(fused_kernel, chips, planes, parts),
         out_shape=(
-            jax.ShapeDtypeStruct((rows, model_width), jnp.bfloat16),
-            jax.ShapeDtypeStruct((local_experts, share, model_width), jnp.float32),
+            jax.ShapeDtypeStruct((planes, 2 * chips, rows, model_width), jnp.bfloat16),
+            jax.ShapeDtypeStruct((planes, local_experts, share, count), jnp.bfloat16),
+            jax.ShapeDtypeStruct((rows, model_width), jnp.float32),
+            jax.ShapeDtypeStruct((chips - 1, rows, model_width), jnp.bfloat16),
         ),
-        in_specs=[pl.BlockSpec(memory_space=pl.ANY)] * 7,
-        out_specs=(vmem, vmem),
+        in_specs=[anywhere] * 7,
+        out_specs=(anywhere,) * 4,
         scratch_shapes=[pltpu.VMEM(dims, kind) for dims, kind in shapes]
         + [
-            pltpu.SemaphoreType.DMA((4 + 3 * local_experts,)),
+            pltpu.SemaphoreType.DMA((5 + 4 * local_experts + parts,)),
             pltpu.SemaphoreType.DMA((amount,)),
             pltpu.SemaphoreType.DMA((amount,)),
         ],
@@ -371,8 +396,30 @@
             collective_id=0, has_side_effects=True, vmem_limit_bytes=60 << 20
         ),
         name="expert_backward",
-    )(tokens, out_grad, routes, route_gates, w_gate, w_up, w_down)
-    return (token_grad, down_grad.transpose(1, 0, 2))
+    )(tokens, out_grad, routes.T, route_gates.T, w_gate, w_up, w_down)
+    width = model_width // STEPS
+    lines = width // 128 * local_experts
+    token_grad, down_grad = pl.pallas_call(
+        finish_kernel,
+        grid=(STEPS,),
+        out_shape=(
+            jax.ShapeDtypeStruct((rows, model_width), jnp.bfloat16),
+            jax.ShapeDtypeStruct((share, model_width // 128 * local_experts, 128), jnp.float32),
+        ),
+        in_specs=[
+            pl.BlockSpec((planes * count, width), lambda i: (0, i)),
+            pl.BlockSpec((planes, local_experts, share, count), lambda i: (0, 0, 0, 0)),
+            pl.BlockSpec((rows, width), lambda i: (0, i)),
+            pl.BlockSpec((chips - 1, rows, width), lambda i: (0, 0, i)),
+        ],
+        out_specs=(
+            pl.BlockSpec((rows, width), lambda i: (0, i)),
+            pl.BlockSpec((share, lines, 128), lambda i: (0, i, 0)),
+        ),
+        name="expert_finish",
+    )(every.reshape(planes * count, model_width), hid, own_sum, returned)
+    down_grad = down_grad.reshape(share, model_width // 128, local_experts, 128)
+    return (token_grad, down_grad.transpose(0, 2, 1, 3).reshape(share, local_experts, model_width))
 
 
 def solution(mesh):

time: 41.6 us -> 32.7 us (0.79)
  local copies, waits for them, and re-layouts: 7.14 us -> 0 us
  Pallas kernels: 33.6 us -> 31.9 us
    unnamed x6 -> x0, local copies, waits for them, and re-layouts: 7.14 us -> none
    pallas_call x1, Pallas kernels: 33.6 us -> 27.5 us  [shards(): pl.pallas_call(functools.partial(fused_kernel, chips, planes, parts), out...]
    pallas_call x0 -> x1, Pallas kernels: none -> 4.38 us  [shards(): pl.pallas_call(finish_kernel, grid=(STEPS,), out_shape=(jax.ShapeDtypeStr...]
where the time goes in v2:
time: 32.7 us; the launch traced here: 32.5 us
  Pallas kernels  31.9 us (98%)
  between operations  0.64 us (2%)
    pallas_call x1, Pallas kernels, shards(): pl.pallas_call(functools.partial(fused_kernel, chips, planes, parts), out...  27.5 us
    pallas_call x1, Pallas kernels, shards(): pl.pallas_call(finish_kernel, grid=(STEPS,), out_shape=(jax.ShapeDtypeStr...  4.38 us

profile of v2, /device:TPU:0, one launch (start us, length us, event | category | flops | bytes accessed | tf_op | source)
XLA Modules:
  0.0 32.5 jit_solution(14914963293191469910)
XLA Ops:
  0.6 27.5 %expert_backward.1 = (bf16[4,8,16,2048]{3,2,1,0:T(8,128)(2,1)}, bf16[4,2,96,128]{3,2,1,0:T(8,128)(2,1)}, f32[16,2048]{1,0:T(8,128)}, bf16[3,16,2048]{2,1,0:T(8,128)(2,1)}) custom-call(bf16[16,2048]{1,0:T(8,128)(2,1)} %tok.1, bf16[16,2048]{1,0:T(8,128)(2,1)} %dy.1, s32[8,16]{1,0:T(8,128)} %bitcast.9, f32[8,16]{1,0:T(8,128)} %bitcast.10, ...), custom_call_target="tpu_custom_call" | custom-call | tf_op jit(solution)/shard_map/expert_backward/pallas_call | solution.py:379
  28.2 4.4 %expert_finish.1 = (bf16[16,2048]{1,0:T(8,128)(2,1)}, f32[96,32,128]{2,1,0:T(8,128)}) custom-call(bf16[512,2048]{1,0:T(8,128)(2,1)} %bitcast.8, bf16[4,2,96,128]{3,2,1,0:T(8,128)(2,1)} %get-tuple-element.9.hid, f32[16,2048]{1,0:T(8,128)} %get-tuple-element.10.own_sum, bf16[3,16,2048]{2,1,0:T(8,128)(2,1)} %get-tuple-element.11.returned), custom_call_target="tpu_custom_call" | custom-call | tf_op jit(solution)/shard_map/expert_finish/pallas_call | solution.py:402

commit v3 on v2

--- a/solution.py
+++ b/solution.py
@@ -8,7 +8,10 @@
 from jax.sharding import PartitionSpec as P
 
 VMEM_BUDGET = 44 << 20
-STEPS = 4
+STEPS = 2
+ALONG = 1
+LAG = 1
+NAMES = ("r", "g", "x0", "x1")
 NT = (((1,), (1,)), ((), ()))
 
 
@@ -99,7 +102,7 @@
 
 def copy_keys(chips, planes, local_experts, parts):
     keys = []
-    for name in ("x", "r", "g"):
+    for name in NAMES:
         keys += [(name, d) for d in range(1, chips)] + [(name + "c", d) for d in range(chips)]
     keys += [("z", k) for k in range(1, planes)]
     keys += [("d", k, d) for k in range(planes) for d in range(1, chips)]
@@ -112,7 +115,7 @@
 
 def fused_kernel(
     chips, planes, parts, tok, dy, rt, gt, wg, wu, wd, every, hid_in, own_sum, ret_in,
-    xb, db, rb, gb, wgv, wuv, wdv, gates, ups, hid_out, grads_g, grads_u,
+    xb, db, rb, gb, wgv, wuv, wdv, gates, ups, grads, hid_out, grads_g, grads_u,
     keep, pair_out, pair_in, ret_out, lsem, ssem, rsem,
 ):
     local_experts, model_width, hidden_units = wg.shape
@@ -147,12 +150,16 @@
         )
 
     copies = {}
-    for name, src, buf in (("x", tok, xb), ("r", rt, rb), ("g", gt, gb)):
+    half = model_width // 2
+    for name in NAMES:
+        src, buf = {"r": (rt, rb), "g": (gt, gb)}.get(name, (tok, xb))
+        cols = pl.ds(int(name[1]) * half, half) if name[0] == "x" else slice(None)
+        src = src.at[:, cols]
         for d in range(chips):
             if d:
-                copies[name, d] = remote((name, d), src, buf.at[2 * d], across[d])
+                copies[name, d] = remote((name, d), src, buf.at[2 * d, :, cols], across[d])
             copies[name + "c", d] = remote(
-                (name + "c", d), buf.at[2 * d] if d else src, buf.at[2 * d + 1], partner
+                (name + "c", d), buf.at[2 * d, :, cols] if d else src, buf.at[2 * d + 1, :, cols], partner
             )
     for k in range(planes):
         blocks = every.at[k] if k else db
@@ -160,7 +167,7 @@
             copies["z", k] = remote(("z", k), dy, blocks.at[0], above[k])
         first = blocks.at[0] if k else dy
         for d in range(chips):
-            if k and d == chips - 1:
+            if 0 < k <= ALONG and d == chips - 1:
                 copies["d", k, d] = remote(("d", k, d), db.at[2 * d], blocks.at[2 * d], above[k])
             elif d:
                 copies["d", k, d] = remote(("d", k, d), first, blocks.at[2 * d], across[d])
@@ -186,103 +193,113 @@
         pl.semaphore_signal(barrier, inc=1, device_id=target, device_id_type=pl.DeviceIdType.MESH)
     pl.semaphore_wait(barrier, len(targets))
 
-    for name in ("x", "r", "g"):
-        for d in range(1, chips):
-            copies[name, d].start()
+    for d in range(chips - 1, 0, -1):
+        copies["d", 0, d].start()
     for k in range(planes - 1, 0, -1):
         copies["z", k].start()
-    for d in range(1, chips):
-        copies["d", 0, d].start()
-    for name in ("x", "r", "g"):
+    for name in NAMES:
+        for d in range(chips - 1, 0, -1):
+            copies[name, d].start()
+    copies["dc", 0, 0].start()
+    for name in NAMES:
         copies[name + "c", 0].start()
-    copies["dc", 0, 0].start()
-
-    for d in range(1, chips):
-        for name in ("x", "r", "g"):
-            copies[name, d].wait_recv()
-            copies[name + "c", d].start()
+    for d in range(chips - 1, 0, -1):
+        copies["d", 0, d].wait_recv()
+        copies["dc", 0, d].start()
+        if d == chips - 1:
+            for k in range(1, min(planes, ALONG + 1)):
+                copies["d", k, d].start()
+    for k in range(1, planes):
+        copies["z", k].wait_recv()
+        for d in range(chips - 1, 0, -1):
+            if d < chips - 1 or k > ALONG:
+                copies["d", k, d].start()
+        copies["dc", k, 0].start()
     for c in own:
         c.wait()
     for d in range(chips):
-        for name in ("x", "r", "g"):
-            copies[name + "c", d].wait_recv()
-
-    x = xb[...].reshape(count, model_width)
-    for e in range(local_experts):
-        for c in gate_up_loads[e]:
-            c.wait()
-        gates[e] = jnp.dot(x, wgv[e], preferred_element_type=jnp.float32)
-        ups[e] = jnp.dot(x, wuv[e], preferred_element_type=jnp.float32)
-        if e == 0:
-            for d in range(1, chips):
-                copies["d", 0, d].wait_recv()
-                copies["dc", 0, d].start()
-            for k in range(1, planes):
-                copies["d", k, chips - 1].start()
-            for k in range(1, planes):
-                copies["z", k].wait_recv()
-                for d in range(1, chips - 1):
-                    copies["d", k, d].start()
-                copies["dc", k, 0].start()
-    for d in range(chips):
         copies["dc", 0, d].wait_recv()
     load(db, every.at[0])
+    grad_rows = db[...].reshape(count, model_width)
+    for e in range(local_experts):
+        down_loads[e].wait()
+        grads[e] = lax.dot_general(grad_rows, wdv[e], NT, preferred_element_type=jnp.float32)
+
+    for name in NAMES:
+        for d in range(chips - 1, 0, -1):
+            copies[name, d].wait_recv()
+            copies[name + "c", d].start()
+    for name in NAMES:
+        for d in range(chips):
+            copies[name + "c", d].wait_recv()
+        if name[0] == "x":
+            begin = int(name[1]) * half
+            x = xb[:, :, begin : begin + half].reshape(count, half)
+            for e in range(local_experts):
+                if begin == 0:
+                    for c in gate_up_loads[e]:
+                        c.wait()
+                for pre, weights in ((gates, wgv), (ups, wuv)):
+                    term = jnp.dot(
+                        x, weights[e, begin : begin + half, :], preferred_element_type=jnp.float32
+                    )
+                    pre[e] = term if begin == 0 else pre[e] + term
 
     named, given = rb[...], gb[...]
     diagonal = lax.broadcasted_iota(jnp.int32, (1, rows, rows), 1) == lax.broadcasted_iota(
         jnp.int32, (1, rows, rows), 2
     )
-    grad_rows = db[...].reshape(count, model_width)
     for e in range(local_experts):
-        down_loads[e].wait()
         gain = jnp.sum(
             jnp.where(named == me * local_experts + e, given, 0.0), axis=1, keepdims=True
         )
         gain = jnp.sum(jnp.where(diagonal, gain, 0.0), axis=2, keepdims=True).reshape(count, 1)
-        hidden_grad = gain * lax.dot_general(
-            grad_rows, wdv[e], NT, preferred_element_type=jnp.float32
-        )
+        hidden_grad = gain * grads[e]
         gate_pre, up_pre = gates[e], ups[e]
         s = jax.nn.sigmoid(gate_pre)
         silu = gate_pre * s
-        hid_out[e] = (silu * up_pre * gain).T.astype(jnp.bfloat16)
+        ups[e] = silu * up_pre * gain
         grads_g[e] = (hidden_grad * up_pre * (s + gate_pre * s * (1.0 - s))).astype(jnp.bfloat16)
         grads_u[e] = (hidden_grad * silu).astype(jnp.bfloat16)
-    for k in range(1, planes):
-        for e in range(local_experts):
-            copies["h", k, e].start()
-    first = pl.multiple_of(plane * share, 16)
-    for e in range(local_experts):
-        load(hid_out.at[e, pl.ds(first, share)], hid_in.at[0, e])
-
-    for j in range(parts):
-        cols = pl.ds(j * width, width)
-        total = None
-        for e in range(local_experts):
-            for grads, weights in ((grads_g, wgv), (grads_u, wuv)):
-                term = lax.dot_general(
-                    grads[e], weights[e, cols, :], NT, preferred_element_type=jnp.float32
-                )
-                total = term if total is None else total + term
-        total = total.reshape(chips, 2, rows, width)
-        keep[j] = total[:, 0]
-        pair_out[j] = total[:, 1].astype(jnp.bfloat16)
-        copies["p", j].start()
+
+    for j in range(parts + LAG):
+        if j < parts:
+            cols = pl.ds(j * width, width)
+            total = None
+            for e in range(local_experts):
+                for rows_grad, weights in ((grads_g, wgv), (grads_u, wuv)):
+                    term = lax.dot_general(
+                        rows_grad[e], weights[e, cols, :], NT, preferred_element_type=jnp.float32
+                    )
+                    total = term if total is None else total + term
+            total = total.reshape(chips, 2, rows, width)
+            pair_out[j] = total[:, 1].astype(jnp.bfloat16)
+            copies["p", j].start()
+            keep[j] = total[:, 0]
+        if j == parts - 1:
+            for e in range(local_experts):
+                hid_out[e] = ups[e].T.astype(jnp.bfloat16)
+            for k in range(1, planes):
+                for e in range(local_experts):
+                    copies["h", k, e].start()
+            first = pl.multiple_of(plane * share, 16)
+            for e in range(local_experts):
+                load(hid_out.at[e, pl.ds(first, share)], hid_in.at[0, e])
+        if j >= LAG:
+            i = j - LAG
+            copies["p", i].wait_recv()
+            total = keep[i] + pair_in[i].astype(jnp.float32)
+            for d in range(chips - 1, 0, -1):
+                ret_out[i, d] = total[d].astype(jnp.bfloat16)
+            for d in range(chips - 1, 0, -1):
+                copies["t", i, d].start()
+            keep[i, 0] = total[0]
+            load(keep.at[i, 0], own_sum.at[:, pl.ds(i * width, width)])
 
     for k in range(1, planes):
         for d in range(1, chips):
             copies["d", k, d].wait_recv()
             copies["dc", k, d].start()
-
-    for j in range(parts):
-        copies["p", j].wait_recv()
-        total = keep[j] + pair_in[j].astype(jnp.float32)
-        keep[j, 0] = total[0]
-        load(keep.at[j, 0], own_sum.at[:, pl.ds(j * width, width)])
-        for d in range(1, chips):
-            ret_out[j, d] = total[d].astype(jnp.bfloat16)
-        for d in range(1, chips):
-            copies["t", j, d].start()
 
     for k in range(1, planes):
         for e in range(local_experts):
@@ -298,21 +315,55 @@
         c.wait_send()
 
 
-def finish_kernel(every, hid, own_sum, returned, token_out, down_out):
-    planes, local_experts, share, _ = hid.shape
-    blocks = every.shape[1] // 128
-    lines = down_out.reshape(share * blocks * local_experts, 128)
-    for e in range(local_experts):
-        pieces = jnp.concatenate([hid[k, e] for k in range(planes)], axis=1)
-        result = jnp.dot(pieces, every[...], preferred_element_type=jnp.float32)
-        for b in range(blocks):
-            lines[pl.ds(b * local_experts + e, share, stride=blocks * local_experts), :] = (
-                result[:, b * 128 : (b + 1) * 128]
-            )
-    total = own_sum[...]
-    for d in range(returned.shape[0]):
-        total = total + returned[d].astype(jnp.float32)
-    token_out[...] = total.astype(jnp.bfloat16)
+def finish_kernel(
+    every, hid, own_sum, returned, token_out, down_out,
+    every_v, hid_v, own_v, returned_v, token_v, down_v, sems,
+):
+    planes, local_experts, share, count = hid.shape
+    width = every.shape[1] // STEPS
+    blocks = width // 128
+    started = []
+
+    def copy(src, dst):
+        c = pltpu.make_async_copy(src, dst, sems.at[len(started)])
+        c.start()
+        started.append(c)
+        return c
+
+    hid_load = copy(hid, hid_v)
+    loads = [
+        copy(every.at[:, pl.ds(i * width, width)], every_v.at[:, pl.ds(i * width, width)])
+        for i in range(STEPS)
+    ]
+    last_loads = [copy(own_sum, own_v), copy(returned, returned_v)]
+    hid_load.wait()
+    pieces = [hid_v[k].reshape(local_experts * share, count) for k in range(planes)]
+    pieces = jnp.concatenate(pieces, axis=1)
+    stores = []
+    for i in range(STEPS):
+        loads[i].wait()
+        result = jnp.dot(
+            pieces, every_v[:, i * width : (i + 1) * width], preferred_element_type=jnp.float32
+        )
+        lines = down_v.at[i].reshape(share * blocks * local_experts, 128)
+        for e in range(local_experts):
+            for b in range(blocks):
+                lines[pl.ds(b * local_experts + e, share, stride=blocks * local_experts), :] = (
+                    result[e * share : (e + 1) * share, b * 128 : (b + 1) * 128]
+                )
+        stores.append(
+            copy(down_v.at[i], down_out.at[:, pl.ds(i * blocks * local_experts, blocks * local_experts)])
+        )
+        if i == 0:
+            for c in last_loads:
+                c.wait()
+            total = own_v[...]
+            for d in range(returned.shape[0]):
+                total = total + returned_v[d].astype(jnp.float32)
+            token_v[...] = total.astype(jnp.bfloat16)
+            stores.append(copy(token_v, token_out))
+    for c in stores:
+        c.wait()
 
 
 def fused_shapes(chips, planes, parts, rows, top, local_experts, model_width, hidden_units):
@@ -326,6 +377,7 @@
         ((local_experts, model_width, hidden_units), bf16),
         ((local_experts, model_width, hidden_units), bf16),
         ((local_experts, hidden_units, model_width), bf16),
+        ((local_experts, count, hidden_units), f32),
         ((local_experts, count, hidden_units), f32),
         ((local_experts, count, hidden_units), f32),
         ((local_experts, hidden_units, count), bf16),
@@ -401,21 +453,22 @@
     lines = width // 128 * local_experts
     token_grad, down_grad = pl.pallas_call(
         finish_kernel,
-        grid=(STEPS,),
         out_shape=(
             jax.ShapeDtypeStruct((rows, model_width), jnp.bfloat16),
             jax.ShapeDtypeStruct((share, model_width // 128 * local_experts, 128), jnp.float32),
         ),
-        in_specs=[
-            pl.BlockSpec((planes * count, width), lambda i: (0, i)),
-            pl.BlockSpec((planes, local_experts, share, count), lambda i: (0, 0, 0, 0)),
-            pl.BlockSpec((rows, width), lambda i: (0, i)),
-            pl.BlockSpec((chips - 1, rows, width), lambda i: (0, 0, i)),
+        in_specs=[anywhere] * 4,
+        out_specs=(anywhere,) * 2,
+        scratch_shapes=[
+            pltpu.VMEM((planes * count, model_width), jnp.bfloat16),
+            pltpu.VMEM(hid.shape, jnp.bfloat16),
+            pltpu.VMEM((rows, model_width), jnp.float32),
+            pltpu.VMEM((chips - 1, rows, model_width), jnp.bfloat16),
+            pltpu.VMEM((rows, model_width), jnp.bfloat16),
+            pltpu.VMEM((STEPS, share, lines, 128), jnp.float32),
+            pltpu.SemaphoreType.DMA((4 + 2 * STEPS,)),
         ],
-        out_specs=(
-            pl.BlockSpec((rows, width), lambda i: (0, i)),
-            pl.BlockSpec((share, lines, 128), lambda i: (0, i, 0)),
-        ),
+        compiler_params=pltpu.CompilerParams(vmem_limit_bytes=60 << 20),
         name="expert_finish",
     )(every.reshape(planes * count, model_width), hid, own_sum, returned)
     down_grad = down_grad.reshape(share, model_width // 128, local_experts, 128)

time: 32.7 us -> 30.2 us (0.924)
  Pallas kernels: 31.9 us -> 29.5 us
    pallas_call x1, Pallas kernels: 27.5 us -> 26.2 us  [shards(): pl.pallas_call(functools.partial(fused_kernel, chips, planes, parts), out...]
    pallas_call x1, Pallas kernels: 4.38 us -> 3.26 us  [shards(): pl.pallas_call(finish_kernel, out_shape=(jax.ShapeDtypeStruct((rows, mode...]
where the time goes in v3:
time: 30.2 us; the launch traced here: 30.1 us
  Pallas kernels  29.5 us (98%)
  between operations  0.64 us (2%)
    pallas_call x1, Pallas kernels, shards(): pl.pallas_call(functools.partial(fused_kernel, chips, planes, parts), out...  26.2 us
    pallas_call x1, Pallas kernels, shards(): pl.pallas_call(finish_kernel, out_shape=(jax.ShapeDtypeStruct((rows, mode...  3.26 us

profile of v3, /device:TPU:0, one launch (start us, length us, event | category | flops | bytes accessed | tf_op | source)
XLA Modules:
  0.0 30.1 jit_solution(7050332234248913959)
XLA Ops:
  0.6 26.2 %expert_backward.1 = (bf16[4,8,16,2048]{3,2,1,0:T(8,128)(2,1)}, bf16[4,2,96,128]{3,2,1,0:T(8,128)(2,1)}, f32[16,2048]{1,0:T(8,128)}, bf16[3,16,2048]{2,1,0:T(8,128)(2,1)}) custom-call(bf16[16,2048]{1,0:T(8,128)(2,1)} %tok.1, bf16[16,2048]{1,0:T(8,128)(2,1)} %dy.1, s32[8,16]{1,0:T(8,128)} %bitcast.9, f32[8,16]{1,0:T(8,128)} %bitcast.10, ...), custom_call_target="tpu_custom_call" | custom-call | tf_op jit(solution)/shard_map/expert_backward/pallas_call | solution.py:431
  26.8 3.3 %expert_finish.1 = (bf16[16,2048]{1,0:T(8,128)(2,1)}, f32[96,32,128]{2,1,0:T(8,128)}) custom-call(bf16[512,2048]{1,0:T(8,128)(2,1)} %bitcast.8, bf16[4,2,96,128]{3,2,1,0:T(8,128)(2,1)} %get-tuple-element.9.hid, f32[16,2048]{1,0:T(8,128)} %get-tuple-element.10.own_sum, bf16[3,16,2048]{2,1,0:T(8,128)(2,1)} %get-tuple-element.11.returned), custom_call_target="tpu_custom_call" | custom-call | tf_op jit(solution)/shard_map/expert_finish/pallas_call | solution.py:454
